TPU v7x, 32 devices: a whole 2x2x4 slice. The times are simulated.
32 devices in a mesh: fsdp: 8 (over y, x, core), seq: 4 (over z).
Axes of the slice: x: 2, y: 2, z: 4, core: 2. Of those that a mesh axis runs over, the one named last changes fastest.
Arguments:
- inputs: bfloat16 [3, 8, 1024, 1024], P(None, 'fsdp', 'seq'), may hold values from -6 to 6
- segment_ids: int32 [3, 8, 1024], P(None, 'fsdp'), may hold values from 0 to 3, never falling along the last dimension, each value on 1 to 512 neighbouring positions
- buckets: int32 [1024], replicated, may hold values from 0 to 31, as said below
- ln1_gain: bfloat16 [1024], P('fsdp'), may hold values from 0.5 to 1.5
- ln1_bias: bfloat16 [1024], P('fsdp'), may hold values from -3 to 3
- w_query: bfloat16 [1024, 1024], P('fsdp'), may hold values from -0.1875 to 0.1875
- w_key: bfloat16 [1024, 1024], P('fsdp'), may hold values from -0.1875 to 0.1875
- w_value: bfloat16 [1024, 1024], P('fsdp'), may hold values from -0.1875 to 0.1875
- w_out: bfloat16 [1024, 1024], P('fsdp'), may hold values from -0.75 to 0.75
- rel_bias: bfloat16 [32, 16], P('fsdp'), may hold values from -4 to 4
- second_norm_gain: bfloat16 [1024], P('fsdp'), may hold values from 0.5 to 1.5
- ln2_bias: bfloat16 [1024], P('fsdp'), may hold values from -3 to 3
- w_up: bfloat16 [1024, 4096], P('fsdp'), may hold values from -0.1875 to 0.1875
- b_up: bfloat16 [4096], P('fsdp'), may hold values from -3 to 3
- w_down: bfloat16 [4096, 1024], P('fsdp'), may hold values from -0.09375 to 0.09375
- b_down: bfloat16 [1024], P('fsdp'), may hold values from -3 to 3
- cotangent: bfloat16 [3, 8, 1024, 1024], P(None, 'fsdp', 'seq'), may hold values from -6 to 6
Outputs:
- outputs: bfloat16 [3, 8, 1024, 1024], P(None, 'fsdp', 'seq')
- input_grad: bfloat16 [3, 8, 1024, 1024], P(None, 'fsdp', 'seq')
- grad_ln1_gain: float32 [1024], P('fsdp')
- grad_ln1_bias: float32 [1024], P('fsdp')
- grad_w_query: float32 [1024, 1024], P('fsdp')
- grad_w_key: float32 [1024, 1024], P('fsdp')
- grad_w_value: float32 [1024, 1024], P('fsdp')
- grad_w_out: float32 [1024, 1024], P('fsdp')
- grad_rel_bias: float32 [32, 16], P('fsdp')
- grad_ln2_gain: float32 [1024], P('fsdp')
- grad_ln2_bias: float32 [1024], P('fsdp')
- grad_w_up: float32 [1024, 4096], P('fsdp')
- grad_b_up: float32 [4096], P('fsdp')
- grad_w_down: float32 [4096, 1024], P('fsdp')
- grad_b_down: float32 [1024], P('fsdp')
Inputs may be any that keep to these rules, and one draw needn't show every extreme that they name: `segment_ids`: along a row the clip number never falls; each clip of a row has 1 to 512 tokens, and some clip has exactly 512. `buckets`: the bucket never falls as the distance grows; it is 0 at distance 0 and 31 at distance 1024 - 1.
All inputs are finite; a program needn't handle non-finite values.
Results may differ from a plain program's by a relative error of at most 0.025.
Values may be sent and summed in bfloat16 or wider, within the bound.
No kernel may reach another device: no remote copies, remote signals or barrier semaphores. Data moves between devices by JAX's collectives and lax.ppermute only.
A program may use at most 448 MiB of HBM per device.

v0:
```python
import jax
import jax.numpy as jnp
from jax import lax
from jax.sharding import PartitionSpec as P

epsilon = 1e-05
masked_out = -1e30
EXACT_PRECISION = lax.Precision.HIGHEST


def layer_norm(field, norm_gain, norm_shift):
    centre = field - jnp.mean(field, axis=-1, keepdims=True)
    spread = jnp.mean(centre * centre, axis=-1, keepdims=True)
    return centre * lax.rsqrt(spread + epsilon) * norm_gain + norm_shift


def gelu_exact(field):
    return jax.nn.gelu(field, approximate=False)


def token_dot(left, right):
    return lax.dot_general(
        left, right, (((0,), (0,)), ((), ())), preferred_element_type=jnp.float32
    )


def back_dot(left, right):
    return lax.dot_general(
        left, right, (((1,), (1,)), ((), ())), preferred_element_type=jnp.float32
    )


def bucket_onehot(distance, first_dist, bucket_ids):
    reached = (distance[None] >= first_dist[:, None, None]).astype(jnp.int32)
    bucket_rows = jnp.sum(reached[1:], axis=0)
    return (bucket_ids[:, None, None] == bucket_rows[None]).astype(jnp.float32)


def per_device(
    inputs,
    segment_ids,
    buckets,
    ln1_gain,
    ln1_bias,
    w_query,
    w_key,
    w_value,
    w_out,
    rel_bias,
    second_norm_gain,
    ln2_bias,
    w_up,
    b_up,
    w_down,
    b_down,
    cotangent,
):
    num_micro, num_rows, local_len, model_width = inputs.shape
    seq_len = segment_ids.shape[2]
    head_count = rel_bias.shape[1]
    head_dim = model_width // head_count
    score_scale = head_dim ** (-0.5)
    num_buckets = rel_bias.shape[0] * lax.axis_size("fsdp")
    num_tokens = num_rows * local_len
    first_pos = lax.axis_index("seq") * local_len
    query_pos = first_pos + jnp.arange(local_len, dtype=jnp.int32)
    key_pos = jnp.arange(seq_len, dtype=jnp.int32)
    distance = query_pos[:, None] - key_pos[None, :]
    causal = distance >= 0
    bucket_ids = jnp.arange(num_buckets, dtype=jnp.int32)
    first_dist = jnp.sum((buckets[None, :] < bucket_ids[:, None]).astype(jnp.int32), axis=1)
    bucket_onehot_matrix = bucket_onehot(distance, first_dist, bucket_ids)
    summed = None
    result_list = []
    grad_list = []
    for micro_step in range(num_micro):
        gathered = (
            lax.all_gather(ln1_gain, "fsdp", axis=0, tiled=True),
            lax.all_gather(ln1_bias, "fsdp", axis=0, tiled=True),
            lax.all_gather(w_query, "fsdp", axis=0, tiled=True),
            lax.all_gather(w_key, "fsdp", axis=0, tiled=True),
            lax.all_gather(w_value, "fsdp", axis=0, tiled=True),
            lax.all_gather(w_out, "fsdp", axis=0, tiled=True),
            lax.all_gather(rel_bias, "fsdp", axis=0, tiled=True),
            lax.all_gather(second_norm_gain, "fsdp", axis=0, tiled=True),
            lax.all_gather(ln2_bias, "fsdp", axis=0, tiled=True),
            lax.all_gather(w_up, "fsdp", axis=0, tiled=True),
            lax.all_gather(b_up, "fsdp", axis=0, tiled=True),
            lax.all_gather(w_down, "fsdp", axis=0, tiled=True),
            lax.all_gather(b_down, "fsdp", axis=0, tiled=True),
        )
        (
            norm1_gain,
            norm1_shift,
            query_mat,
            key_mat,
            value_mat,
            out_mat,
            rel_table,
            norm2_gain,
            norm2_shift,
            up_mat,
            up_bias,
            down_mat,
            down_bias,
        ) = gathered
        relative_float_bias = rel_table.astype(jnp.float32)
        score_position_bias = jnp.einsum(
            "uia,uw->wia", bucket_onehot_matrix, relative_float_bias, precision=EXACT_PRECISION
        )
        row_x = inputs[micro_step].reshape(num_tokens, model_width).astype(jnp.float32)
        normed_one, norm1_pull = jax.vjp(
            layer_norm, row_x, norm1_gain.astype(jnp.float32), norm1_shift.astype(jnp.float32)
        )
        normed_low = normed_one.astype(jnp.bfloat16)
        queries = jnp.dot(normed_low, query_mat, preferred_element_type=jnp.float32).astype(
            jnp.bfloat16
        )
        keys_local = jnp.dot(normed_low, key_mat, preferred_element_type=jnp.float32).astype(
            jnp.bfloat16
        )
        values_local = jnp.dot(normed_low, value_mat, preferred_element_type=jnp.float32).astype(
            jnp.bfloat16
        )
        keys_all, values_all = (
            lax.all_gather(
                keys_local.reshape(num_rows, local_len, model_width), "seq", axis=1, tiled=True
            ),
            lax.all_gather(
                values_local.reshape(num_rows, local_len, model_width), "seq", axis=1, tiled=True
            ),
        )
        row_segment_ids = segment_ids[micro_step]
        query_segs = lax.dynamic_slice_in_dim(row_segment_ids, first_pos, local_len, 1)
        seg_mask = (query_segs[:, :, None] == row_segment_ids[:, None, :]) & causal[None]
        query_four = queries.reshape(num_rows, local_len, head_count, head_dim)
        keys_four = keys_all.reshape(num_rows, seq_len, head_count, head_dim)
        values_four = values_all.reshape(num_rows, seq_len, head_count, head_dim)

        def make_logits():
            raw_scores = (
                jnp.einsum(
                    "rqhd,rkhd->rhqk", query_four, keys_four, preferred_element_type=jnp.float32
                )
                * score_scale
                + score_position_bias[None]
            )
            return jnp.where(seg_mask[:, None], raw_scores, masked_out)

        logits = make_logits()
        row_peak = jnp.max(logits, axis=-1, keepdims=True)
        expo = jnp.exp(logits - row_peak)
        row_total = jnp.sum(expo, axis=-1, keepdims=True)
        soft_probs = expo / row_total
        log_total = row_peak + jnp.log(row_total)
        attended = jnp.einsum(
            "rhqk,rkhd->rqhd",
            soft_probs.astype(jnp.bfloat16),
            values_four,
            preferred_element_type=jnp.float32,
        )
        attended = attended.reshape(num_tokens, model_width).astype(jnp.bfloat16)
        middle = row_x + jnp.dot(attended, out_mat, preferred_element_type=jnp.float32)
        normed_two, norm2_pull = jax.vjp(
            layer_norm, middle, norm2_gain.astype(jnp.float32), norm2_shift.astype(jnp.float32)
        )
        normed_two_low = normed_two.astype(jnp.bfloat16)
        pre_act = jnp.dot(
            normed_two_low, up_mat, preferred_element_type=jnp.float32
        ) + up_bias.astype(jnp.float32)
        activation, gelu_pull = jax.vjp(gelu_exact, pre_act)
        activation_low = activation.astype(jnp.bfloat16)
        result_row = (
            middle
            + jnp.dot(activation_low, down_mat, preferred_element_type=jnp.float32)
            + down_bias.astype(jnp.float32)
        )
        result_list.append(
            result_row.astype(jnp.bfloat16).reshape(num_rows, local_len, model_width)
        )
        grad_out = cotangent[micro_step].reshape(num_tokens, model_width)
        grad_out_f = grad_out.astype(jnp.float32)
        grad_w_down = token_dot(activation_low, grad_out)
        grad_b_down = jnp.sum(grad_out_f, axis=0)
        grad_act = back_dot(grad_out, down_mat)
        grad_pre = gelu_pull(grad_act)[0].astype(jnp.bfloat16)
        grad_b_up = jnp.sum(grad_pre.astype(jnp.float32), axis=0)
        grad_w_up = token_dot(normed_two_low, grad_pre)
        grad_norm2 = back_dot(grad_pre, up_mat)
        grad_mid_norm, grad_ln2_gain, grad_ln2_bias = norm2_pull(grad_norm2)
        grad_middle = grad_out_f + grad_mid_norm
        grad_branch = grad_middle.astype(jnp.bfloat16)
        grad_w_out = token_dot(attended, grad_branch)
        grad_attended = (
            back_dot(grad_branch, out_mat)
            .astype(jnp.bfloat16)
            .reshape(num_rows, local_len, head_count, head_dim)
        )
        again_probs = jnp.exp(make_logits() - log_total)
        grad_probs = jnp.einsum(
            "rqhd,rkhd->rhqk", grad_attended, values_four, preferred_element_type=jnp.float32
        )
        row_delta = jnp.sum(grad_probs * again_probs, axis=-1, keepdims=True)
        grad_scores = (again_probs * (grad_probs - row_delta)).astype(jnp.bfloat16)
        grad_queries = (
            jnp.einsum(
                "rhqk,rkhd->rqhd", grad_scores, keys_four, preferred_element_type=jnp.float32
            )
            * score_scale
        ).astype(jnp.bfloat16)
        grad_rel = jnp.einsum(
            "vlp,glp->vg",
            bucket_onehot_matrix,
            jnp.sum(grad_scores.astype(jnp.float32), axis=0),
            precision=EXACT_PRECISION,
        )
        grad_values = jnp.einsum(
            "rhqk,rqhd->rkhd",
            again_probs.astype(jnp.bfloat16),
            grad_attended,
            preferred_element_type=jnp.float32,
        )
        grad_keys = (
            jnp.einsum(
                "rhqk,rqhd->rkhd", grad_scores, query_four, preferred_element_type=jnp.float32
            )
            * score_scale
        )
        key_grads, value_grads = (
            lax.psum_scatter(
                grad_keys.reshape(num_rows, seq_len, model_width).astype(jnp.bfloat16),
                "seq",
                scatter_dimension=1,
                tiled=True,
            ).astype(jnp.float32),
            lax.psum_scatter(
                grad_values.reshape(num_rows, seq_len, model_width).astype(jnp.bfloat16),
                "seq",
                scatter_dimension=1,
                tiled=True,
            ).astype(jnp.float32),
        )
        key_grads = key_grads.astype(jnp.bfloat16).reshape(num_tokens, model_width)
        value_grads = value_grads.astype(jnp.bfloat16).reshape(num_tokens, model_width)
        grad_queries = grad_queries.reshape(num_tokens, model_width)
        grad_w_query = token_dot(normed_low, grad_queries)
        grad_w_key = token_dot(normed_low, key_grads)
        grad_w_value = token_dot(normed_low, value_grads)
        gradient_first_norm = (
            back_dot(grad_queries, query_mat)
            + back_dot(key_grads, key_mat)
            + back_dot(value_grads, value_mat)
        )
        grad_x_norm, grad_ln1_gain, grad_ln1_bias = norm1_pull(gradient_first_norm)
        grad_list.append(
            (grad_middle + grad_x_norm)
            .astype(jnp.bfloat16)
            .reshape(num_rows, local_len, model_width)
        )
        local_grads = (
            grad_ln1_gain,
            grad_ln1_bias,
            grad_w_query,
            grad_w_key,
            grad_w_value,
            grad_w_out,
            grad_rel,
            grad_ln2_gain,
            grad_ln2_bias,
            grad_w_up,
            grad_b_up,
            grad_w_down,
            grad_b_down,
        )
        shard_part = (
            lax.psum_scatter(
                local_grads[0].astype(jnp.bfloat16), "fsdp", scatter_dimension=0, tiled=True
            ).astype(jnp.float32),
            lax.psum_scatter(
                local_grads[1].astype(jnp.bfloat16), "fsdp", scatter_dimension=0, tiled=True
            ).astype(jnp.float32),
            lax.psum_scatter(
                local_grads[2].astype(jnp.bfloat16), "fsdp", scatter_dimension=0, tiled=True
            ).astype(jnp.float32),
            lax.psum_scatter(
                local_grads[3].astype(jnp.bfloat16), "fsdp", scatter_dimension=0, tiled=True
            ).astype(jnp.float32),
            lax.psum_scatter(
                local_grads[4].astype(jnp.bfloat16), "fsdp", scatter_dimension=0, tiled=True
            ).astype(jnp.float32),
            lax.psum_scatter(
                local_grads[5].astype(jnp.bfloat16), "fsdp", scatter_dimension=0, tiled=True
            ).astype(jnp.float32),
            lax.psum_scatter(
                local_grads[6].astype(jnp.bfloat16), "fsdp", scatter_dimension=0, tiled=True
            ).astype(jnp.float32),
            lax.psum_scatter(
                local_grads[7].astype(jnp.bfloat16), "fsdp", scatter_dimension=0, tiled=True
            ).astype(jnp.float32),
            lax.psum_scatter(
                local_grads[8].astype(jnp.bfloat16), "fsdp", scatter_dimension=0, tiled=True
            ).astype(jnp.float32),
            lax.psum_scatter(
                local_grads[9].astype(jnp.bfloat16), "fsdp", scatter_dimension=0, tiled=True
            ).astype(jnp.float32),
            lax.psum_scatter(
                local_grads[10].astype(jnp.bfloat16), "fsdp", scatter_dimension=0, tiled=True
            ).astype(jnp.float32),
            lax.psum_scatter(
                local_grads[11].astype(jnp.bfloat16), "fsdp", scatter_dimension=0, tiled=True
            ).astype(jnp.float32),
            lax.psum_scatter(
                local_grads[12].astype(jnp.bfloat16), "fsdp", scatter_dimension=0, tiled=True
            ).astype(jnp.float32),
        )
        summed = shard_part if summed is None else jax.tree.map(jnp.add, summed, shard_part)
    totals = (
        lax.psum(summed[0].astype(jnp.bfloat16), "seq").astype(jnp.float32),
        lax.psum(summed[1].astype(jnp.bfloat16), "seq").astype(jnp.float32),
        lax.psum(summed[2].astype(jnp.bfloat16), "seq").astype(jnp.float32),
        lax.psum(summed[3].astype(jnp.bfloat16), "seq").astype(jnp.float32),
        lax.psum(summed[4].astype(jnp.bfloat16), "seq").astype(jnp.float32),
        lax.psum(summed[5].astype(jnp.bfloat16), "seq").astype(jnp.float32),
        lax.psum(summed[6].astype(jnp.bfloat16), "seq").astype(jnp.float32),
        lax.psum(summed[7].astype(jnp.bfloat16), "seq").astype(jnp.float32),
        lax.psum(summed[8].astype(jnp.bfloat16), "seq").astype(jnp.float32),
        lax.psum(summed[9].astype(jnp.bfloat16), "seq").astype(jnp.float32),
        lax.psum(summed[10].astype(jnp.bfloat16), "seq").astype(jnp.float32),
        lax.psum(summed[11].astype(jnp.bfloat16), "seq").astype(jnp.float32),
        lax.psum(summed[12].astype(jnp.bfloat16), "seq").astype(jnp.float32),
    )
    return (
        jnp.stack(result_list),
        jnp.stack(grad_list),
        totals[0],
        totals[1],
        totals[2],
        totals[3],
        totals[4],
        totals[5],
        totals[6],
        totals[7],
        totals[8],
        totals[9],
        totals[10],
        totals[11],
        totals[12],
    )


def solution(mesh):
    return jax.shard_map(
        per_device,
        mesh=mesh,
        in_specs=(
            P(None, "fsdp", "seq", None),
            P(None, "fsdp", None),
            P(),
            P("fsdp"),
            P("fsdp"),
            P("fsdp", None),
            P("fsdp", None),
            P("fsdp", None),
            P("fsdp", None),
            P("fsdp", None),
            P("fsdp"),
            P("fsdp"),
            P("fsdp", None),
            P("fsdp"),
            P("fsdp", None),
            P("fsdp"),
            P(None, "fsdp", "seq", None),
        ),
        out_specs=(
            P(None, "fsdp", "seq", None),
            P(None, "fsdp", "seq", None),
            P("fsdp"),
            P("fsdp"),
            P("fsdp", None),
            P("fsdp", None),
            P("fsdp", None),
            P("fsdp", None),
            P("fsdp", None),
            P("fsdp"),
            P("fsdp"),
            P("fsdp", None),
            P("fsdp"),
            P("fsdp", None),
            P("fsdp"),
        ),
        check_vma=False,
    )
```

profile of v0, /device:TPU:0, one launch (start us, length us, event | category | flops | bytes accessed | tf_op | source)
XLA Modules:
  0.0 2055.5 jit_solution(9363248587604546310)
XLA Ops:
  197.7 43.8 %all-gather.46.cloned.1.call-done = bf16[1024,1024]{1,0:T(8,128)(2,1)} async-done(((bf16[256,1024]{1,0:T(8,128)(2,1)}), bf16[1024,1024]{1,0:T(8,128)(2,1)}) %all-gather.46.cloned.1.call-update) | async-done | bytes 2097168 | tf_op jit(solution)/shard_map/all_gather | solution.py:129
  245.5 42.9 %all-gather.38.cloned.1.call-done = bf16[1024,1024]{1,0:T(8,128)(2,1)} async-done(((bf16[256,1024]{1,0:T(8,128)(2,1)}), bf16[1024,1024]{1,0:T(8,128)(2,1)}) %all-gather.38.cloned.1.call-update) | async-done | bytes 2097168 | tf_op jit(solution)/shard_map/all_gather | solution.py:129
  593.6 41.8 %reduce-scatter.25.cloned.1.call-done = bf16[1,256,1024]{1,2,0:T(8,128)(2,1)} async-done(((bf16[1,1024,1024]{1,2,0:T(8,128)(2,1)}), bf16[1,256,1024]{1,2,0:T(8,128)(2,1)}) %reduce-scatter.25.cloned.1.call-update) | async-done | bytes 524304 | tf_op jit(solution)/shard_map/reduce_scatter | solution.py:230
  638.9 42.0 %reduce-scatter.27.cloned.1.call-done = bf16[1,256,1024]{1,2,0:T(8,128)(2,1)} async-done(((bf16[1,1024,1024]{1,2,0:T(8,128)(2,1)}), bf16[1,256,1024]{1,2,0:T(8,128)(2,1)}) %reduce-scatter.27.cloned.1.call-update) | async-done | bytes 524304 | tf_op jit(solution)/shard_map/reduce_scatter | solution.py:236
  693.6 39.5 %all-gather.44.cloned.1.call-done = bf16[1024,1024]{1,0:T(8,128)(2,1)} async-done(((bf16[256,1024]{1,0:T(8,128)(2,1)}), bf16[1024,1024]{1,0:T(8,128)(2,1)}) %all-gather.44.cloned.1.call-update) | async-done | bytes 2097168 | tf_op jit(solution)/shard_map/all_gather | solution.py:126
  897.1 27.6 %reduce-scatter.29.cloned.1.call-done = bf16[1,256,1024]{1,2,0:T(8,128)(2,1)} async-done(((bf16[1,1024,1024]{1,2,0:T(8,128)(2,1)}), bf16[1,256,1024]{1,2,0:T(8,128)(2,1)}) %reduce-scatter.29.cloned.1.call-update) | async-done | bytes 524304 | tf_op jit(solution)/shard_map/reduce_scatter | solution.py:230
  1033.5 24.4 %reduce-scatter.57.cloned.1.call-done = bf16[128,1024]{1,0:T(8,128)(2,1)} async-done(((bf16[1024,1024]{1,0:T(8,128)(2,1)}), bf16[128,1024]{1,0:T(8,128)(2,1)}) %reduce-scatter.57.cloned.1.call-update) | async-done | bytes 262160 | tf_op jit(solution)/shard_map/reduce_scatter | solution.py:291
  1059.8 42.9 %reduce-scatter.41.cloned.1.call-done = bf16[128,1024]{1,0:T(8,128)(2,1)} async-done(((bf16[1024,1024]{1,0:T(8,128)(2,1)}), bf16[128,1024]{1,0:T(8,128)(2,1)}) %reduce-scatter.41.cloned.1.call-update) | async-done | bytes 262160 | tf_op jit(solution)/shard_map/reduce_scatter | solution.py:282
  1102.7 44.5 %reduce-scatter.37.cloned.1.call-done = bf16[128,1024]{1,0:T(8,128)(2,1)} async-done(((bf16[1024,1024]{1,0:T(8,128)(2,1)}), bf16[128,1024]{1,0:T(8,128)(2,1)}) %reduce-scatter.37.cloned.1.call-update) | async-done | bytes 262160 | tf_op jit(solution)/shard_map/reduce_scatter | solution.py:282
  1147.2 44.7 %reduce-scatter.39.cloned.1.call-done = bf16[128,1024]{1,0:T(8,128)(2,1)} async-done(((bf16[1024,1024]{1,0:T(8,128)(2,1)}), bf16[128,1024]{1,0:T(8,128)(2,1)}) %reduce-scatter.39.cloned.1.call-update) | async-done | bytes 262160 | tf_op jit(solution)/shard_map/reduce_scatter | solution.py:282
  1197.7 38.8 %reduce-scatter.49.cloned.1.call-done = bf16[128,1024]{1,0:T(8,128)(2,1)} async-done(((bf16[1024,1024]{1,0:T(8,128)(2,1)}), bf16[128,1024]{1,0:T(8,128)(2,1)}) %reduce-scatter.49.cloned.1.call-update) | async-done | bytes 262160 | tf_op jit(solution)/shard_map/reduce_scatter | solution.py:288
  1236.5 44.7 %reduce-scatter.53.cloned.1.call-done = bf16[128,1024]{1,0:T(8,128)(2,1)} async-done(((bf16[1024,1024]{1,0:T(8,128)(2,1)}), bf16[128,1024]{1,0:T(8,128)(2,1)}) %reduce-scatter.53.cloned.1.call-update) | async-done | bytes 262160 | tf_op jit(solution)/shard_map/reduce_scatter | solution.py:288
  1281.3 44.4 %reduce-scatter.51.cloned.1.call-done = bf16[128,1024]{1,0:T(8,128)(2,1)} async-done(((bf16[1024,1024]{1,0:T(8,128)(2,1)}), bf16[128,1024]{1,0:T(8,128)(2,1)}) %reduce-scatter.51.cloned.1.call-update) | async-done | bytes 262160 | tf_op jit(solution)/shard_map/reduce_scatter | solution.py:288
  1327.6 43.0 %reduce-scatter.47.cloned.1.call-done = bf16[128,1024]{1,0:T(8,128)(2,1)} async-done(((bf16[1024,1024]{1,0:T(8,128)(2,1)}), bf16[128,1024]{1,0:T(8,128)(2,1)}) %reduce-scatter.47.cloned.1.call-update) | async-done | bytes 262160 | tf_op jit(solution)/shard_map/reduce_scatter | solution.py:285
  1370.5 44.5 %reduce-scatter.43.cloned.1.call-done = bf16[128,1024]{1,0:T(8,128)(2,1)} async-done(((bf16[1024,1024]{1,0:T(8,128)(2,1)}), bf16[128,1024]{1,0:T(8,128)(2,1)}) %reduce-scatter.43.cloned.1.call-update) | async-done | bytes 262160 | tf_op jit(solution)/shard_map/reduce_scatter | solution.py:285
  1415.1 44.7 %reduce-scatter.45.cloned.1.call-done = bf16[128,1024]{1,0:T(8,128)(2,1)} async-done(((bf16[1024,1024]{1,0:T(8,128)(2,1)}), bf16[128,1024]{1,0:T(8,128)(2,1)}) %reduce-scatter.45.cloned.1.call-update) | async-done | bytes 262160 | tf_op jit(solution)/shard_map/reduce_scatter | solution.py:285
  1461.7 72.8 %reduce-scatter.65.cloned.1.call-done = bf16[128,4096]{1,0:T(8,128)(2,1)} async-done(((bf16[1024,4096]{1,0:T(8,128)(2,1)}), bf16[128,4096]{1,0:T(8,128)(2,1)}) %reduce-scatter.65.cloned.1.call-update) | async-done | bytes 1048592 | tf_op jit(solution)/shard_map/reduce_scatter | solution.py:303
  1534.6 75.2 %reduce-scatter.61.cloned.1.call-done = bf16[128,4096]{1,0:T(8,128)(2,1)} async-done(((bf16[1024,4096]{1,0:T(8,128)(2,1)}), bf16[128,4096]{1,0:T(8,128)(2,1)}) %reduce-scatter.61.cloned.1.call-update) | async-done | bytes 1048592 | tf_op jit(solution)/shard_map/reduce_scatter | solution.py:303
  1609.8 74.6 %reduce-scatter.63.cloned.1.call-done = bf16[128,4096]{1,0:T(8,128)(2,1)} async-done(((bf16[1024,4096]{1,0:T(8,128)(2,1)}), bf16[128,4096]{1,0:T(8,128)(2,1)}) %reduce-scatter.63.cloned.1.call-update) | async-done | bytes 1048592 | tf_op jit(solution)/shard_map/reduce_scatter | solution.py:303
  1687.7 71.9 %reduce-scatter.71.cloned.1.call-done = bf16[512,1024]{1,0:T(8,128)(2,1)} async-done(((bf16[4096,1024]{1,0:T(8,128)(2,1)}), bf16[512,1024]{1,0:T(8,128)(2,1)}) %reduce-scatter.71.cloned.1.call-update) | async-done | bytes 1048592 | tf_op jit(solution)/shard_map/reduce_scatter | solution.py:309
  1759.6 74.8 %reduce-scatter.67.cloned.1.call-done = bf16[512,1024]{1,0:T(8,128)(2,1)} async-done(((bf16[4096,1024]{1,0:T(8,128)(2,1)}), bf16[512,1024]{1,0:T(8,128)(2,1)}) %reduce-scatter.67.cloned.1.call-update) | async-done | bytes 1048592 | tf_op jit(solution)/shard_map/reduce_scatter | solution.py:309
  1834.3 75.0 %reduce-scatter.69.cloned.1.call-done = bf16[512,1024]{1,0:T(8,128)(2,1)} async-done(((bf16[4096,1024]{1,0:T(8,128)(2,1)}), bf16[512,1024]{1,0:T(8,128)(2,1)}) %reduce-scatter.69.cloned.1.call-update) | async-done | bytes 1048592 | tf_op jit(solution)/shard_map/reduce_scatter | solution.py:309
  1919.6 25.7 %all-reduce.21 = (bf16[1024]{0:T(1024)(128)(2,1)S(1)}, bf16[1024]{0:T(1024)(128)(2,1)S(1)}, bf16[1024]{0:T(1024)(128)(2,1)S(1)}, bf16[1024]{0:T(1024)(128)(2,1)S...) all-reduce(bf16[1024]{0:T(1024)(128)(2,1)S(1)} %get-tuple-element.1, ...), channel_id=16, replica_groups=mesh['fsdp'=8,'seq'=4] {'fsdp'}, use_global_device_ids=true, to_apply=%region_46.47.clone | all-reduce | flops 29184 | bytes 116736
  1966.4 70.2 %all-reduce.26.cloned.1.call-done = (bf16[128,1024]{1,0:T(8,128)(2,1)}, bf16[128,1024]{1,0:T(8,128)(2,1)}, bf16[128,1024]{1,0:T(8,128)(2,1)}, bf16[128,1024]{1,0...) async-done(((bf16[128,1024]{1,0:T(8,128)(2,1)}, bf16[128,1024]{1,0:T(8,128)(2,1)}, bf16[128,1024]{1,0:T(8,128)(2,1)}, bf16[128,1024]{1,0:T(8,128)(2,1)}, ...) | async-done | bytes 3145744 | tf_op jit(solution)/shard_map/psum | solution.py:320
  (623 shorter events, 841.6 us)
Async XLA Ops:
  47.1 194.4 %all-gather.46.cloned.1.call-start = ((), (), s32[]{:S(2)}) async-start(), calls=%async_computation.58 | async-start | bytes 2621440 | tf_op jit(solution)/shard_map/all_gather | solution.py:129
  73.6 214.8 %all-gather.38.cloned.1.call-start = ((), (), s32[]{:S(2)}) async-start(), calls=%async_computation.54 | async-start | bytes 2621440 | tf_op jit(solution)/shard_map/all_gather | solution.py:129
  76.8 240.1 %all-gather.32.cloned.1.call-start = ((), (), s32[]{:S(2)}) async-start(), calls=%async_computation.27 | async-start | bytes 2359296 | tf_op jit(solution)/shard_map/all_gather | solution.py:83
  77.5 295.7 %all-gather.34.cloned.1.call-start = ((), (), s32[]{:S(2)}) async-start(), calls=%async_computation.28 | async-start | bytes 9437184 | tf_op jit(solution)/shard_map/all_gather | solution.py:87
  78.3 351.1 %all-gather.36.cloned.1.call-start = ((), (), s32[]{:S(2)}) async-start(), calls=%async_computation.29 | async-start | bytes 9437184 | tf_op jit(solution)/shard_map/all_gather | solution.py:89
  78.8 489.5 %reduce-scatter.33.cloned.1.call-start = ((), (), s32[]{:S(2)}) async-start(), calls=%async_computation.34 | async-start | bytes 2621440 | tf_op jit(solution)/shard_map/reduce_scatter | solution.py:230
  690.9 197.3 %reduce-scatter.31.cloned.1.call-start = ((), (), s32[]{:S(2)}) async-start(), calls=%async_computation.33 | async-start | bytes 2621440 | tf_op jit(solution)/shard_map/reduce_scatter | solution.py:236
  862.8 195.1 %reduce-scatter.57.cloned.1.call-start = ((), (), s32[]{:S(2)}) async-start(), calls=%async_computation.46 | async-start | bytes 2359296 | tf_op jit(solution)/shard_map/reduce_scatter | solution.py:291
  864.9 237.8 %reduce-scatter.41.cloned.1.call-start = ((), (), s32[]{:S(2)}) async-start(), calls=%async_computation.38 | async-start | bytes 2359296 | tf_op jit(solution)/shard_map/reduce_scatter | solution.py:282
  868.2 279.0 %reduce-scatter.37.cloned.1.call-start = ((), (), s32[]{:S(2)}) async-start(), calls=%async_computation.36 | async-start | bytes 2359296 | tf_op jit(solution)/shard_map/reduce_scatter | solution.py:282
  871.9 320.1 %reduce-scatter.39.cloned.1.call-start = ((), (), s32[]{:S(2)}) async-start(), calls=%async_computation.37 | async-start | bytes 2359296 | tf_op jit(solution)/shard_map/reduce_scatter | solution.py:282
  882.5 354.0 %reduce-scatter.49.cloned.1.call-start = ((), (), s32[]{:S(2)}) async-start(), calls=%async_computation.42 | async-start | bytes 2359296 | tf_op jit(solution)/shard_map/reduce_scatter | solution.py:288
  885.9 395.4 %reduce-scatter.53.cloned.1.call-start = ((), (), s32[]{:S(2)}) async-start(), calls=%async_computation.44 | async-start | bytes 2359296 | tf_op jit(solution)/shard_map/reduce_scatter | solution.py:288
  888.2 437.5 %reduce-scatter.51.cloned.1.call-start = ((), (), s32[]{:S(2)}) async-start(), calls=%async_computation.43 | async-start | bytes 2359296 | tf_op jit(solution)/shard_map/reduce_scatter | solution.py:288
  891.5 479.0 %reduce-scatter.47.cloned.1.call-start = ((), (), s32[]{:S(2)}) async-start(), calls=%async_computation.41 | async-start | bytes 2359296 | tf_op jit(solution)/shard_map/reduce_scatter | solution.py:285
  893.8 521.3 %reduce-scatter.43.cloned.1.call-start = ((), (), s32[]{:S(2)}) async-start(), calls=%async_computation.39 | async-start | bytes 2359296 | tf_op jit(solution)/shard_map/reduce_scatter | solution.py:285
  897.1 562.7 %reduce-scatter.45.cloned.1.call-start = ((), (), s32[]{:S(2)}) async-start(), calls=%async_computation.40 | async-start | bytes 2359296 | tf_op jit(solution)/shard_map/reduce_scatter | solution.py:285
  928.0 606.6 %reduce-scatter.65.cloned.1.call-start = ((), (), s32[]{:S(2)}) async-start(), calls=%async_computation.50 | async-start | bytes 9437184 | tf_op jit(solution)/shard_map/reduce_scatter | solution.py:303
  935.8 673.9 %reduce-scatter.61.cloned.1.call-start = ((), (), s32[]{:S(2)}) async-start(), calls=%async_computation.48 | async-start | bytes 9437184 | tf_op jit(solution)/shard_map/reduce_scatter | solution.py:303
  944.4 740.0 %reduce-scatter.63.cloned.1.call-start = ((), (), s32[]{:S(2)}) async-start(), calls=%async_computation.49 | async-start | bytes 9437184 | tf_op jit(solution)/shard_map/reduce_scatter | solution.py:303
  952.5 807.0 %reduce-scatter.71.cloned.1.call-start = ((), (), s32[]{:S(2)}) async-start(), calls=%async_computation.53 | async-start | bytes 9437184 | tf_op jit(solution)/shard_map/reduce_scatter | solution.py:309
  961.3 873.1 %reduce-scatter.67.cloned.1.call-start = ((), (), s32[]{:S(2)}) async-start(), calls=%async_computation.51 | async-start | bytes 9437184 | tf_op jit(solution)/shard_map/reduce_scatter | solution.py:309
  968.8 940.6 %reduce-scatter.69.cloned.1.call-start = ((), (), s32[]{:S(2)}) async-start(), calls=%async_computation.52 | async-start | bytes 9437184 | tf_op jit(solution)/shard_map/reduce_scatter | solution.py:309
  976.2 1060.4 %all-reduce.26.cloned.1.call-start = ((), (), s32[]{:S(2)}) async-start(), calls=%async_computation.60 | async-start | bytes 6291456 | tf_op jit(solution)/shard_map/psum | solution.py:320
  (185 other events, 6866.7 us)
Sparse Core Ops, SparseCore 0:
  102.2 45.9 all-gather.47
  150.1 44.6 all-gather.39
  196.8 44.6 all-gather.45
  243.7 44.6 all-gather.37
  318.8 54.3 all-gather.33
  374.9 54.3 all-gather.35
  500.5 43.6 reduce-scatter.32
  546.5 43.2 reduce-scatter.34
  592.1 43.1 reduce-scatter.24
  637.6 43.1 reduce-scatter.26
  687.8 45.2 all-gather.43
  735.1 44.6 all-gather.41
  836.7 42.4 reduce-scatter.30
  881.5 43.1 reduce-scatter.28
  972.0 41.2 reduce-scatter.58
  1061.5 41.2 reduce-scatter.40
  1240.0 41.2 reduce-scatter.52
  1463.3 71.2 reduce-scatter.64
  1538.4 71.2 reduce-scatter.60
  1613.1 71.2 reduce-scatter.62
  1688.2 71.2 reduce-scatter.70
  1763.0 71.2 reduce-scatter.66
  1838.0 71.2 reduce-scatter.68
  1913.2 123.3 all-reduce.25
  (13 shorter events, 482.4 us)
where the time goes:
time: 2060 us
  waiting for transfers between devices  1320 us (64%)
  matrix products  479 us (23%)
  blocking collectives  99.5 us (5%)
  other arithmetic  98.5 us (5%)
  local copies, waits for them, and re-layouts  42 us (2%)
    reduce_scatter x3, waiting for transfers between devices, per_device(): lax.psum_scatter(local_grads[9].astype(jnp.bfloat16), 'fsdp', scatter_dim...  223 us
    reduce_scatter x3, waiting for transfers between devices, per_device(): lax.psum_scatter(local_grads[11].astype(jnp.bfloat16), 'fsdp', scatter_di...  222 us
    reduce_scatter x3, waiting for transfers between devices, per_device(): lax.psum_scatter(local_grads[3].astype(jnp.bfloat16), 'fsdp', scatter_dim...  132 us
    reduce_scatter x3, waiting for transfers between devices, per_device(): lax.psum_scatter(local_grads[2].astype(jnp.bfloat16), 'fsdp', scatter_dim...  132 us
    reduce_scatter x3, waiting for transfers between devices, per_device(): lax.psum_scatter(local_grads[4].astype(jnp.bfloat16), 'fsdp', scatter_dim...  128 us
    all_gather x3, waiting for transfers between devices, per_device(): lax.all_gather(values_local.reshape(num_rows, local_len, model_width), 's...  100 us
    dot_general x18, matrix products, back_dot(): lax.dot_general(left, right, (((1,), (1,)), ((), ())), preferred_element_...  84.1 us
    dot_general x18, matrix products, token_dot(): lax.dot_general(left, right, (((0,), (0,)), ((), ())), preferred_element_...  78.6 us
  transfers between devices with their start and end apart: 37, of which 32 were waited for; matrix products, arithmetic and copies ran while one was open for 22% of the time, Pallas kernels for 0%

commit v1 on v0

--- a/solution.py
+++ b/solution.py
@@ -317,7 +317,7 @@
     totals = (
         lax.psum(summed[0].astype(jnp.bfloat16), "seq").astype(jnp.float32),
         lax.psum(summed[1].astype(jnp.bfloat16), "seq").astype(jnp.float32),
-        lax.psum(summed[2].astype(jnp.bfloat16), "seq").astype(jnp.float32),
+        jnp.sum(lax.all_gather(summed[2].astype(jnp.bfloat16), "seq"), axis=0).astype(jnp.float32),
         lax.psum(summed[3].astype(jnp.bfloat16), "seq").astype(jnp.float32),
         lax.psum(summed[4].astype(jnp.bfloat16), "seq").astype(jnp.float32),
         lax.psum(summed[5].astype(jnp.bfloat16), "seq").astype(jnp.float32),

time: 2060 us -> 2080 us (level)
    reduce_scatter x3, waiting for transfers between devices: 24.4 us -> 132 us  [per_device(): lax.psum_scatter(local_grads[5].astype(jnp.bfloat16), 'fsdp', scatter_dim...]
    reduce_scatter x3, waiting for transfers between devices: 132 us -> 24.9 us  [per_device(): lax.psum_scatter(local_grads[2].astype(jnp.bfloat16), 'fsdp', scatter_dim...]
  transfers between devices with their start and end apart: 37 -> 38, of which waited for: 32 -> 32; matrix products, arithmetic and copies ran while one was open for 22% -> 22% of each run, Pallas kernels for 0% -> 0%
where the time goes in v1:
time: 2080 us
  waiting for transfers between devices  1340 us (64%)
  matrix products  480 us (23%)
  blocking collectives  99 us (5%)
  other arithmetic  98.9 us (5%)
  local copies, waits for them, and re-layouts  41.6 us (2%)
    reduce_scatter x3, waiting for transfers between devices, per_device(): lax.psum_scatter(local_grads[11].astype(jnp.bfloat16), 'fsdp', scatter_di...  223 us
    reduce_scatter x3, waiting for transfers between devices, per_device(): lax.psum_scatter(local_grads[9].astype(jnp.bfloat16), 'fsdp', scatter_dim...  221 us
    reduce_scatter x3, waiting for transfers between devices, per_device(): lax.psum_scatter(local_grads[3].astype(jnp.bfloat16), 'fsdp', scatter_dim...  132 us
    reduce_scatter x3, waiting for transfers between devices, per_device(): lax.psum_scatter(local_grads[5].astype(jnp.bfloat16), 'fsdp', scatter_dim...  132 us
    reduce_scatter x3, waiting for transfers between devices, per_device(): lax.psum_scatter(local_grads[4].astype(jnp.bfloat16), 'fsdp', scatter_dim...  128 us
    all_gather x3, waiting for transfers between devices, per_device(): lax.all_gather(values_local.reshape(num_rows, local_len, model_width), 's...  100 us
    psum x1, waiting for transfers between devices, per_device(): lax.psum(summed[3].astype(jnp.bfloat16), 'seq').astype(jnp.float32)  89.2 us
    dot_general x18, matrix products, back_dot(): lax.dot_general(left, right, (((1,), (1,)), ((), ())), preferred_element_...  88.8 us
  transfers between devices with their start and end apart: 38, of which 32 were waited for; matrix products, arithmetic and copies ran while one was open for 22% of the time, Pallas kernels for 0%

profile of v1, /device:TPU:0, one launch (start us, length us, event | category | flops | bytes accessed | tf_op | source)
XLA Modules:
  0.0 2077.6 jit_solution(7250930133436004529)
XLA Ops:
  197.7 43.8 %all-gather.48.cloned.1.call-done = bf16[1024,1024]{1,0:T(8,128)(2,1)} async-done(((bf16[256,1024]{1,0:T(8,128)(2,1)}), bf16[1024,1024]{1,0:T(8,128)(2,1)}) %all-gather.48.cloned.1.call-update) | async-done | bytes 2097168 | tf_op jit(solution)/shard_map/all_gather | solution.py:129
  245.5 42.9 %all-gather.40.cloned.1.call-done = bf16[1024,1024]{1,0:T(8,128)(2,1)} async-done(((bf16[256,1024]{1,0:T(8,128)(2,1)}), bf16[1024,1024]{1,0:T(8,128)(2,1)}) %all-gather.40.cloned.1.call-update) | async-done | bytes 2097168 | tf_op jit(solution)/shard_map/all_gather | solution.py:129
  593.6 41.7 %reduce-scatter.25.cloned.1.call-done = bf16[1,256,1024]{1,2,0:T(8,128)(2,1)} async-done(((bf16[1,1024,1024]{1,2,0:T(8,128)(2,1)}), bf16[1,256,1024]{1,2,0:T(8,128)(2,1)}) %reduce-scatter.25.cloned.1.call-update) | async-done | bytes 524304 | tf_op jit(solution)/shard_map/reduce_scatter | solution.py:230
  638.8 42.0 %reduce-scatter.27.cloned.1.call-done = bf16[1,256,1024]{1,2,0:T(8,128)(2,1)} async-done(((bf16[1,1024,1024]{1,2,0:T(8,128)(2,1)}), bf16[1,256,1024]{1,2,0:T(8,128)(2,1)}) %reduce-scatter.27.cloned.1.call-update) | async-done | bytes 524304 | tf_op jit(solution)/shard_map/reduce_scatter | solution.py:236
  693.5 39.6 %all-gather.46.cloned.1.call-done = bf16[1024,1024]{1,0:T(8,128)(2,1)} async-done(((bf16[256,1024]{1,0:T(8,128)(2,1)}), bf16[1024,1024]{1,0:T(8,128)(2,1)}) %all-gather.46.cloned.1.call-update) | async-done | bytes 2097168 | tf_op jit(solution)/shard_map/all_gather | solution.py:126
  898.7 30.0 %reduce-scatter.29.cloned.1.call-done = bf16[1,256,1024]{1,2,0:T(8,128)(2,1)} async-done(((bf16[1,1024,1024]{1,2,0:T(8,128)(2,1)}), bf16[1,256,1024]{1,2,0:T(8,128)(2,1)}) %reduce-scatter.29.cloned.1.call-update) | async-done | bytes 524304 | tf_op jit(solution)/shard_map/reduce_scatter | solution.py:230
  1037.0 24.9 %reduce-scatter.39.cloned.1.call-done = bf16[128,1024]{1,0:T(8,128)(2,1)} async-done(((bf16[1024,1024]{1,0:T(8,128)(2,1)}), bf16[128,1024]{1,0:T(8,128)(2,1)}) %reduce-scatter.39.cloned.1.call-update) | async-done | bytes 262160 | tf_op jit(solution)/shard_map/reduce_scatter | solution.py:282
  1064.2 42.6 %reduce-scatter.55.cloned.1.call-done = bf16[128,1024]{1,0:T(8,128)(2,1)} async-done(((bf16[1024,1024]{1,0:T(8,128)(2,1)}), bf16[128,1024]{1,0:T(8,128)(2,1)}) %reduce-scatter.55.cloned.1.call-update) | async-done | bytes 262160 | tf_op jit(solution)/shard_map/reduce_scatter | solution.py:291
  1106.8 44.5 %reduce-scatter.59.cloned.1.call-done = bf16[128,1024]{1,0:T(8,128)(2,1)} async-done(((bf16[1024,1024]{1,0:T(8,128)(2,1)}), bf16[128,1024]{1,0:T(8,128)(2,1)}) %reduce-scatter.59.cloned.1.call-update) | async-done | bytes 262160 | tf_op jit(solution)/shard_map/reduce_scatter | solution.py:291
  1151.4 44.7 %reduce-scatter.57.cloned.1.call-done = bf16[128,1024]{1,0:T(8,128)(2,1)} async-done(((bf16[1024,1024]{1,0:T(8,128)(2,1)}), bf16[128,1024]{1,0:T(8,128)(2,1)}) %reduce-scatter.57.cloned.1.call-update) | async-done | bytes 262160 | tf_op jit(solution)/shard_map/reduce_scatter | solution.py:291
  1201.8 38.9 %reduce-scatter.49.cloned.1.call-done = bf16[128,1024]{1,0:T(8,128)(2,1)} async-done(((bf16[1024,1024]{1,0:T(8,128)(2,1)}), bf16[128,1024]{1,0:T(8,128)(2,1)}) %reduce-scatter.49.cloned.1.call-update) | async-done | bytes 262160 | tf_op jit(solution)/shard_map/reduce_scatter | solution.py:288
  1240.6 44.7 %reduce-scatter.53.cloned.1.call-done = bf16[128,1024]{1,0:T(8,128)(2,1)} async-done(((bf16[1024,1024]{1,0:T(8,128)(2,1)}), bf16[128,1024]{1,0:T(8,128)(2,1)}) %reduce-scatter.53.cloned.1.call-update) | async-done | bytes 262160 | tf_op jit(solution)/shard_map/reduce_scatter | solution.py:288
  1285.4 44.4 %reduce-scatter.51.cloned.1.call-done = bf16[128,1024]{1,0:T(8,128)(2,1)} async-done(((bf16[1024,1024]{1,0:T(8,128)(2,1)}), bf16[128,1024]{1,0:T(8,128)(2,1)}) %reduce-scatter.51.cloned.1.call-update) | async-done | bytes 262160 | tf_op jit(solution)/shard_map/reduce_scatter | solution.py:288
  1331.7 42.9 %reduce-scatter.47.cloned.1.call-done = bf16[128,1024]{1,0:T(8,128)(2,1)} async-done(((bf16[1024,1024]{1,0:T(8,128)(2,1)}), bf16[128,1024]{1,0:T(8,128)(2,1)}) %reduce-scatter.47.cloned.1.call-update) | async-done | bytes 262160 | tf_op jit(solution)/shard_map/reduce_scatter | solution.py:285
  1374.6 44.5 %reduce-scatter.43.cloned.1.call-done = bf16[128,1024]{1,0:T(8,128)(2,1)} async-done(((bf16[1024,1024]{1,0:T(8,128)(2,1)}), bf16[128,1024]{1,0:T(8,128)(2,1)}) %reduce-scatter.43.cloned.1.call-update) | async-done | bytes 262160 | tf_op jit(solution)/shard_map/reduce_scatter | solution.py:285
  1419.2 44.7 %reduce-scatter.45.cloned.1.call-done = bf16[128,1024]{1,0:T(8,128)(2,1)} async-done(((bf16[1024,1024]{1,0:T(8,128)(2,1)}), bf16[128,1024]{1,0:T(8,128)(2,1)}) %reduce-scatter.45.cloned.1.call-update) | async-done | bytes 262160 | tf_op jit(solution)/shard_map/reduce_scatter | solution.py:285
  1465.8 72.8 %reduce-scatter.71.cloned.1.call-done = bf16[512,1024]{1,0:T(8,128)(2,1)} async-done(((bf16[4096,1024]{1,0:T(8,128)(2,1)}), bf16[512,1024]{1,0:T(8,128)(2,1)}) %reduce-scatter.71.cloned.1.call-update) | async-done | bytes 1048592 | tf_op jit(solution)/shard_map/reduce_scatter | solution.py:309
  1538.7 75.2 %reduce-scatter.67.cloned.1.call-done = bf16[512,1024]{1,0:T(8,128)(2,1)} async-done(((bf16[4096,1024]{1,0:T(8,128)(2,1)}), bf16[512,1024]{1,0:T(8,128)(2,1)}) %reduce-scatter.67.cloned.1.call-update) | async-done | bytes 1048592 | tf_op jit(solution)/shard_map/reduce_scatter | solution.py:309
  1613.8 74.6 %reduce-scatter.69.cloned.1.call-done = bf16[512,1024]{1,0:T(8,128)(2,1)} async-done(((bf16[4096,1024]{1,0:T(8,128)(2,1)}), bf16[512,1024]{1,0:T(8,128)(2,1)}) %reduce-scatter.69.cloned.1.call-update) | async-done | bytes 1048592 | tf_op jit(solution)/shard_map/reduce_scatter | solution.py:309
  1691.9 71.7 %reduce-scatter.65.cloned.1.call-done = bf16[128,4096]{1,0:T(8,128)(2,1)} async-done(((bf16[1024,4096]{1,0:T(8,128)(2,1)}), bf16[128,4096]{1,0:T(8,128)(2,1)}) %reduce-scatter.65.cloned.1.call-update) | async-done | bytes 1048592 | tf_op jit(solution)/shard_map/reduce_scatter | solution.py:303
  1763.6 74.8 %reduce-scatter.61.cloned.1.call-done = bf16[128,4096]{1,0:T(8,128)(2,1)} async-done(((bf16[1024,4096]{1,0:T(8,128)(2,1)}), bf16[128,4096]{1,0:T(8,128)(2,1)}) %reduce-scatter.61.cloned.1.call-update) | async-done | bytes 1048592 | tf_op jit(solution)/shard_map/reduce_scatter | solution.py:303
  1838.3 75.0 %reduce-scatter.63.cloned.1.call-done = bf16[128,4096]{1,0:T(8,128)(2,1)} async-done(((bf16[1024,4096]{1,0:T(8,128)(2,1)}), bf16[128,4096]{1,0:T(8,128)(2,1)}) %reduce-scatter.63.cloned.1.call-update) | async-done | bytes 1048592 | tf_op jit(solution)/shard_map/reduce_scatter | solution.py:303
  1923.3 25.3 %all-reduce.21 = (bf16[1024]{0:T(1024)(128)(2,1)S(1)}, bf16[1024]{0:T(1024)(128)(2,1)S(1)}, bf16[1024]{0:T(1024)(128)(2,1)S(1)}, bf16[1024]{0:T(1024)(128)(2,1)S...) all-reduce(bf16[1024]{0:T(1024)(128)(2,1)S(1)} %get-tuple-element.1, ...), channel_id=17, replica_groups=mesh['fsdp'=8,'seq'=4] {'fsdp'}, use_global_device_ids=true, to_apply=%region_46.47.clone | all-reduce | flops 29184 | bytes 116736
  1971.7 89.2 %all-reduce.26.cloned.1.call-done = (bf16[128,1024]{1,0:T(8,128)(2,1)}, bf16[128,1024]{1,0:T(8,128)(2,1)}, bf16[128,1024]{1,0:T(8,128)(2,1)}, bf16[128,4096]{1,0:T(8,128)(2,1)}, bf16[512,1024]{1,0:T(8,128)(2,1)}) async-done(((bf16[128,1024]{1,0:T(8,128)(2,1)}, bf16[128,1024]{1,0:T(8,128)(2,1)}, bf16[128,1024]{1,0:T(8,128)(2,1)}, bf16[128,4096]{1,0:T(8,128)(2,1)}, bf16[512,1024]{1,0:T(8,128)(2,1)}), ...) | async-done | bytes 2883600 | tf_op jit(solution)/shard_map/psum | solution.py:321
  (610 shorter events, 843.2 us)
Async XLA Ops:
  47.1 194.4 %all-gather.48.cloned.1.call-start = ((), (), s32[]{:S(2)}) async-start(), calls=%async_computation.58 | async-start | bytes 2621440 | tf_op jit(solution)/shard_map/all_gather | solution.py:129
  73.6 214.8 %all-gather.40.cloned.1.call-start = ((), (), s32[]{:S(2)}) async-start(), calls=%async_computation.54 | async-start | bytes 2621440 | tf_op jit(solution)/shard_map/all_gather | solution.py:129
  76.8 240.1 %all-gather.34.cloned.1.call-start = ((), (), s32[]{:S(2)}) async-start(), calls=%async_computation.27 | async-start | bytes 2359296 | tf_op jit(solution)/shard_map/all_gather | solution.py:83
  77.5 295.7 %all-gather.36.cloned.1.call-start = ((), (), s32[]{:S(2)}) async-start(), calls=%async_computation.28 | async-start | bytes 9437184 | tf_op jit(solution)/shard_map/all_gather | solution.py:87
  78.3 351.1 %all-gather.38.cloned.1.call-start = ((), (), s32[]{:S(2)}) async-start(), calls=%async_computation.29 | async-start | bytes 9437184 | tf_op jit(solution)/shard_map/all_gather | solution.py:89
  78.8 489.4 %reduce-scatter.33.cloned.1.call-start = ((), (), s32[]{:S(2)}) async-start(), calls=%async_computation.34 | async-start | bytes 2621440 | tf_op jit(solution)/shard_map/reduce_scatter | solution.py:230
  690.9 199.9 %reduce-scatter.31.cloned.1.call-start = ((), (), s32[]{:S(2)}) async-start(), calls=%async_computation.33 | async-start | bytes 2621440 | tf_op jit(solution)/shard_map/reduce_scatter | solution.py:236
  879.3 227.5 %reduce-scatter.55.cloned.1.call-start = ((), (), s32[]{:S(2)}) async-start(), calls=%async_computation.45 | async-start | bytes 2359296 | tf_op jit(solution)/shard_map/reduce_scatter | solution.py:291
  881.4 269.9 %reduce-scatter.59.cloned.1.call-start = ((), (), s32[]{:S(2)}) async-start(), calls=%async_computation.47 | async-start | bytes 2359296 | tf_op jit(solution)/shard_map/reduce_scatter | solution.py:291
  883.6 312.6 %reduce-scatter.57.cloned.1.call-start = ((), (), s32[]{:S(2)}) async-start(), calls=%async_computation.46 | async-start | bytes 2359296 | tf_op jit(solution)/shard_map/reduce_scatter | solution.py:291
  886.1 354.5 %reduce-scatter.49.cloned.1.call-start = ((), (), s32[]{:S(2)}) async-start(), calls=%async_computation.42 | async-start | bytes 2359296 | tf_op jit(solution)/shard_map/reduce_scatter | solution.py:288
  888.4 397.0 %reduce-scatter.53.cloned.1.call-start = ((), (), s32[]{:S(2)}) async-start(), calls=%async_computation.44 | async-start | bytes 2359296 | tf_op jit(solution)/shard_map/reduce_scatter | solution.py:288
  890.7 439.0 %reduce-scatter.51.cloned.1.call-start = ((), (), s32[]{:S(2)}) async-start(), calls=%async_computation.43 | async-start | bytes 2359296 | tf_op jit(solution)/shard_map/reduce_scatter | solution.py:288
  894.1 480.5 %reduce-scatter.47.cloned.1.call-start = ((), (), s32[]{:S(2)}) async-start(), calls=%async_computation.41 | async-start | bytes 2359296 | tf_op jit(solution)/shard_map/reduce_scatter | solution.py:285
  896.4 522.8 %reduce-scatter.43.cloned.1.call-start = ((), (), s32[]{:S(2)}) async-start(), calls=%async_computation.39 | async-start | bytes 2359296 | tf_op jit(solution)/shard_map/reduce_scatter | solution.py:285
  898.7 565.2 %reduce-scatter.45.cloned.1.call-start = ((), (), s32[]{:S(2)}) async-start(), calls=%async_computation.40 | async-start | bytes 2359296 | tf_op jit(solution)/shard_map/reduce_scatter | solution.py:285
  932.0 606.7 %reduce-scatter.71.cloned.1.call-start = ((), (), s32[]{:S(2)}) async-start(), calls=%async_computation.53 | async-start | bytes 9437184 | tf_op jit(solution)/shard_map/reduce_scatter | solution.py:309
  939.4 674.4 %reduce-scatter.67.cloned.1.call-start = ((), (), s32[]{:S(2)}) async-start(), calls=%async_computation.51 | async-start | bytes 9437184 | tf_op jit(solution)/shard_map/reduce_scatter | solution.py:309
  946.9 741.5 %reduce-scatter.69.cloned.1.call-start = ((), (), s32[]{:S(2)}) async-start(), calls=%async_computation.52 | async-start | bytes 9437184 | tf_op jit(solution)/shard_map/reduce_scatter | solution.py:309
  954.4 809.2 %reduce-scatter.65.cloned.1.call-start = ((), (), s32[]{:S(2)}) async-start(), calls=%async_computation.50 | async-start | bytes 9437184 | tf_op jit(solution)/shard_map/reduce_scatter | solution.py:303
  962.8 875.5 %reduce-scatter.61.cloned.1.call-start = ((), (), s32[]{:S(2)}) async-start(), calls=%async_computation.48 | async-start | bytes 9437184 | tf_op jit(solution)/shard_map/reduce_scatter | solution.py:303
  971.2 942.1 %reduce-scatter.63.cloned.1.call-start = ((), (), s32[]{:S(2)}) async-start(), calls=%async_computation.49 | async-start | bytes 9437184 | tf_op jit(solution)/shard_map/reduce_scatter | solution.py:303
  979.7 989.7 %all-gather.52.cloned.1.call-start = ((), (), s32[]{:S(2)}) async-start(), calls=%async_computation.60 | async-start | bytes 1310720 | tf_op jit(solution)/shard_map/all_gather | solution.py:320
  1063.9 997.0 %all-reduce.26.cloned.1.call-start = ((), (), s32[]{:S(2)}) async-start(), calls=%async_computation.61 | async-start | bytes 5767168 | tf_op jit(solution)/shard_map/psum | solution.py:321
  (178 other events, 5684.7 us)
Sparse Core Ops, SparseCore 0:
  102.2 45.9 all-gather.49
  150.1 44.6 all-gather.41
  196.8 44.6 all-gather.47
  243.7 44.6 all-gather.39
  318.8 54.3 all-gather.35
  374.9 54.3 all-gather.37
  500.5 43.7 reduce-scatter.32
  546.6 43.1 reduce-scatter.34
  592.1 43.1 reduce-scatter.24
  637.6 43.1 reduce-scatter.26
  687.8 45.2 all-gather.45
  735.1 44.6 all-gather.43
  840.7 42.5 reduce-scatter.30
  885.5 43.1 reduce-scatter.28
  976.1 41.3 reduce-scatter.36
  1154.9 41.2 reduce-scatter.56
  1333.4 41.2 reduce-scatter.46
  1467.4 71.2 reduce-scatter.70
  1542.5 71.2 reduce-scatter.66
  1617.1 71.2 reduce-scatter.68
  1692.3 71.2 reduce-scatter.64
  1767.0 71.2 reduce-scatter.60
  1842.0 71.2 reduce-scatter.62
  1947.2 113.6 all-reduce.25
  (14 shorter events, 510.3 us)
